TPU v7x, 32 devices: a whole 2x2x4 slice. The times are simulated.
32 devices in a mesh: groups: 2 (over x), seq: 16 (over z, y, core).
Axes of the slice: x: 2, y: 2, z: 4, core: 2. Of those that a mesh axis runs over, the one named last changes fastest.
Arguments:
- queries: bfloat16 [4, 2048, 4096], P('groups', 'seq'), parts along dimension 0, may hold values from -120 to 120
- key_states: bfloat16 [4, 2048, 4096], P('groups', 'seq'), parts along dimension 0, may hold values from -4 to 4
- value_states: bfloat16 [4, 2048, 4096], P('groups', 'seq'), parts along dimension 0, may hold values from -6 to 6
- random_blocks: int32 [4, 32, 3], P('groups'), parts along dimension 0, may hold values from 0 to 31
- global_blocks: int32 [4, 2], P('groups'), parts along dimension 0, may hold values from 0 to 31, as said below
Outputs:
- attended: bfloat16 [4, 2048, 4096], P('groups', 'seq'), parts along dimension 0
There are 2 independent parts, one for each index of `groups`. A program takes and returns all parts, laid end to end along the dimension named above; each array names one. Nothing has to cross between parts.
Inputs may be any that keep to these rules, and one draw needn't show every extreme that they name: `global_blocks`: the 2 global blocks of a document are different, the first below 16 and the second not.
All inputs are finite; a program needn't handle non-finite values.
Results may differ from a plain program's by a relative error of at most 0.008.
Values may be sent and summed in bfloat16 or wider, within the bound.
A program may use at most 128 MiB of HBM per device.

v0:
```python
import math

import jax
import jax.numpy as jnp
from jax import lax
from jax.sharding import PartitionSpec as P

HEAD_DIM = 128
BLOCK = 64
NGLOB = 2
NRAND = 3


def from_partner(block, axis, distance):
    count = lax.axis_size(axis)
    route = []
    for low in range(count):
        high = low | 1 << distance
        if high != low and high < count:
            route += [(low, high), (high, low)]
    return lax.ppermute(block, axis, route)


def soft_weights(scores):
    row_max = jnp.max(scores, axis=-1, keepdims=True)
    exponent = jnp.exp(scores - row_max)
    return (exponent / jnp.sum(exponent, axis=-1, keepdims=True)).astype(jnp.bfloat16)


def global_rows(query_rows, key_tokens, value_tokens):
    scores = jnp.einsum(
        "qhs,khs->hqk", query_rows, key_tokens, preferred_element_type=jnp.float32
    ) * HEAD_DIM ** (-0.5)
    weights = soft_weights(scores)
    return jnp.einsum(
        "hqk,khs->qhs", weights, value_tokens, preferred_element_type=jnp.float32
    ).astype(jnp.bfloat16)


def per_device(queries, key_states, value_states, random_blocks, global_blocks):
    devices = lax.axis_size("seq")
    device = lax.axis_index("seq")
    documents = queries.shape[0]
    head_groups = devices // (2 * documents)
    group_width = queries.shape[2] // head_groups
    heads_here = group_width // HEAD_DIM
    block_len = BLOCK
    total_blocks = 2 * devices
    parity = device % 2
    document = device // (2 * head_groups)

    def by_parity(states):
        pieces = states.reshape(documents, 2, block_len, head_groups, group_width)
        return pieces.transpose(0, 3, 1, 2, 4).reshape(devices, block_len, group_width)

    query_recv, key_half, value_half = (
        lax.all_to_all(by_parity(queries), "seq", split_axis=0, concat_axis=1, tiled=True),
        lax.all_to_all(by_parity(key_states), "seq", split_axis=0, concat_axis=1, tiled=True),
        lax.all_to_all(by_parity(value_states), "seq", split_axis=0, concat_axis=1, tiled=True),
    )
    key_other, value_other = from_partner((key_half, value_half), "seq", 0)

    def alternate(own_rows, their_rows):
        own_rows = own_rows.reshape(devices, 1, block_len, group_width)
        their_rows = their_rows.reshape(devices, 1, block_len, group_width)
        joined = jnp.where(
            parity == 0,
            jnp.concatenate([own_rows, their_rows], axis=1),
            jnp.concatenate([their_rows, own_rows], axis=1),
        )
        return joined.reshape(total_blocks * block_len, group_width)

    key_flat = alternate(key_half, key_other)
    value_flat = alternate(value_half, value_other)
    key_blocks = key_flat.reshape(total_blocks, block_len, heads_here, HEAD_DIM)
    value_blocks = value_flat.reshape(total_blocks, block_len, heads_here, HEAD_DIM)
    key_tokens = key_flat.reshape(total_blocks * block_len, heads_here, HEAD_DIM)
    value_tokens = value_flat.reshape(total_blocks * block_len, heads_here, HEAD_DIM)
    query_mine = query_recv.reshape(devices, block_len, heads_here, HEAD_DIM)
    document_lists = lax.dynamic_index_in_dim(random_blocks, document, 0, keepdims=False)
    own_lists = lax.dynamic_index_in_dim(
        document_lists.reshape(devices, 2, NRAND), parity, 1, keepdims=False
    )
    globals_here = lax.dynamic_index_in_dim(global_blocks, document, 0, keepdims=False)
    positions = 2 * jnp.arange(devices, dtype=jnp.int32) + parity
    listed = jnp.concatenate(
        [
            jnp.broadcast_to(globals_here[None, :], (devices, NGLOB)),
            (positions - 1)[:, None],
            positions[:, None],
            (positions + 1)[:, None],
            own_lists,
        ],
        axis=1,
    )
    live_mask = jnp.concatenate(
        [
            jnp.ones((devices, NGLOB), jnp.bool_),
            (positions >= 1)[:, None],
            jnp.ones((devices, 1), jnp.bool_),
            (positions + 1 < total_blocks)[:, None],
            jnp.ones((devices, NRAND), jnp.bool_),
        ],
        axis=1,
    )
    listed = jnp.clip(listed, 0, total_blocks - 1)
    per_step = math.gcd(devices, max(1, 512 // block_len))
    step_count = devices // per_step

    def local_group(packed):
        query_group, listed_group, live_group = packed
        gathered_keys = jnp.take(key_blocks, listed_group, axis=0).reshape(
            per_step, -1, heads_here, HEAD_DIM
        )
        gathered_values = jnp.take(value_blocks, listed_group, axis=0).reshape(
            per_step, -1, heads_here, HEAD_DIM
        )
        scores = jnp.einsum(
            "pqhs,pkhs->phqk", query_group, gathered_keys, preferred_element_type=jnp.float32
        ) * HEAD_DIM ** (-0.5)
        live_tokens = jnp.repeat(live_group, block_len, axis=1)
        scores = jnp.where(live_tokens[:, None, None, :], scores, -1e30)
        weights = soft_weights(scores)
        return jnp.einsum(
            "phqk,pkhs->pqhs", weights, gathered_values, preferred_element_type=jnp.float32
        ).astype(jnp.bfloat16)

    attended = lax.map(
        local_group,
        (
            query_mine.reshape(step_count, per_step, block_len, heads_here, HEAD_DIM),
            listed.reshape(step_count, per_step, -1),
            live_mask.reshape(step_count, per_step, -1),
        ),
    )
    attended = attended.reshape(devices, block_len, heads_here, HEAD_DIM)
    owned = [globals_here[slot_index] % 2 == parity for slot_index in range(NGLOB)]
    places = [globals_here[slot_index] // 2 for slot_index in range(NGLOB)]
    for slot_index in range(NGLOB):
        place_here = places[slot_index]

        def compute_rows(current):
            rows_here = lax.dynamic_index_in_dim(query_mine, place_here, 0, keepdims=False)
            return lax.dynamic_update_index_in_dim(
                current, global_rows(rows_here, key_tokens, value_tokens), place_here, 0
            )

        def keep_rows(current):
            return current

        attended = lax.cond(owned[slot_index], compute_rows, keep_rows, attended)
    returned = lax.all_to_all(
        attended.reshape(devices, block_len, group_width),
        "seq",
        split_axis=0,
        concat_axis=0,
        tiled=True,
    )
    returned = returned.reshape(documents, head_groups, 2, block_len, group_width).transpose(
        0, 2, 3, 1, 4
    )
    return returned.reshape(documents, 2 * block_len, head_groups * group_width)


def solution(mesh):
    placed = (
        P("groups", "seq", None),
        P("groups", "seq", None),
        P("groups", "seq", None),
        P("groups", None, None),
        P("groups", None),
    )
    return jax.shard_map(
        per_device, mesh=mesh, in_specs=placed, out_specs=P("groups", "seq", None), check_vma=False
    )
```

profile of v0, /device:TPU:1, one launch (start us, length us, event | category | flops | bytes accessed | tf_op | source)
XLA Modules:
  0.0 424.9 jit_solution(15134097178231390452)
XLA Ops:
  17.9 36.3 %all-to-all-done = bf16[16,64,1024]{2,1,0:T(8,128)(2,1)} async-done(((bf16[16,64,1024]{2,1,0:T(8,128)(2,1)}), bf16[16,64,1024]{2,1,0:T(8,128)(2,1)}, u32[]{:S(2)}, u32[]{:S(2)}) %all-to-all-start) | async-done | bytes 2097184 | tf_op jit(solution)/shard_map/all_to_all | solution.py:59
  54.3 10.7 %all-to-all-start.2 = ((bf16[16,64,1024]{2,1,0:T(8,128)(2,1)}), bf16[16,64,1024]{2,1,0:T(8,128)(2,1)}, u32[]{:S(2)}, u32[]{:S(2)}) async-start(bf16[16,64,1024]{2,1,0:T(8,128)(2,1)} %bitcast.26), calls=%async_computation.2 | async-start | bytes 4194304 | tf_op jit(solution)/shard_map/all_to_all | solution.py:58
  70.3 36.3 %all-to-all-done.2 = bf16[16,64,1024]{2,1,0:T(8,128)(2,1)} async-done(((bf16[16,64,1024]{2,1,0:T(8,128)(2,1)}), bf16[16,64,1024]{2,1,0:T(8,128)(2,1)}, u32[]{:S(2)}, u32[]{:S(2)}) %all-to-all-start.2) | async-done | bytes 2097184 | tf_op jit(solution)/shard_map/all_to_all | solution.py:58
  106.6 10.7 %all-to-all-start.1 = ((bf16[16,64,1024]{2,1,0:T(8,128)(2,1)}), bf16[16,64,1024]{2,1,0:T(8,128)(2,1)S(1)}, u32[]{:S(2)}, u32[]{:S(2)}) async-start(bf16[16,64,1024]{2,1,0:T(8,128)(2,1)} %bitcast.24), calls=%async_computation.1 | async-start | bytes 4194304 | tf_op jit(solution)/shard_map/all_to_all | solution.py:57
  123.0 35.8 %all-to-all-done.1 = bf16[16,64,1024]{2,1,0:T(8,128)(2,1)S(1)} async-done(((bf16[16,64,1024]{2,1,0:T(8,128)(2,1)}), bf16[16,64,1024]{2,1,0:T(8,128)(2,1)S(1)}, u32[]{:S(2)}, u32[]{:S(2)}) %all-to-all-start.1) | async-done | bytes 2097184 | tf_op jit(solution)/shard_map/all_to_all | solution.py:57
  175.6 149.2 %while.10 = (s32[]{:T(128)}, bf16[2,8,64,8,128]{4,2,3,1,0:T(8,128)(2,1)}, s32[2,8,8]{1,0,2:T(2,128)S(1)}, bf16[32,64,8,128]{3,2,1,0:T(8,128)(2,1)}, pred[2,8,8]{...) while((s32[]{:T(128)}, ...), condition=%wide.region_3.5_spmd, body=%wide.region_0.4_spmd.sunk | while | flops 1099433984 | bytes 155246496 | solution.py:128
  175.8 7.6 %gather_fusion = bf16[64,64,8,128]{3,2,1,0:T(8,128)(2,1)} fusion(bf16[32,64,8,128]{3,2,1,0:T(8,128)(2,1)} %get-tuple-element.278, s32[1024]{0:T(1024)S(1)} %pad_clamp_fusion.2), kind=kCustom, calls=%fused_computation.1.clone.clone.1 | custom fusion | bytes 16777472 | tf_op jit(solution)/shard_map/while/body/eval_jaxpr/jit(_take)/gather | solution.py:112
  183.4 7.6 %gather_fusion.1 = bf16[64,64,8,128]{3,2,1,0:T(8,128)(2,1)} fusion(bf16[32,64,8,128]{3,2,1,0:T(8,128)(2,1)} %get-tuple-element.275, s32[1024]{0:T(1024)S(1)} %pad_clamp_fusion.2), kind=kCustom, calls=%fused_computation.clone.clone.1 | custom fusion | bytes 16777472 | tf_op jit(solution)/shard_map/while/body/eval_jaxpr/jit(_take)/gather | solution.py:115
  191.0 11.6 %broadcast_select_fusion.3 = (bf16[8,8,64,8,128]{4,3,2,1,0:T(8,128)(2,1)}, bf16[8,8,64,8,128]{4,3,2,1,0:T(8,128)(2,1)}) fusion(bf16[8,8,64,8,128]{4,3,2,1,0:T(8,128)(2,1)} %bitcast.131, pred[8,8]{1,0:T(8,128)(4,1)S(1)} %compare_and_fusion.2, bf16[8,8,64,8,128]{4,3,2,1,0:T(8,128)(2,1)} %bitcast.132), kind=kLoop, calls=%fused_computation.46.clone.1 | loop fusion | flops 8388608 | bytes 33554496 | tf_op jit(solution)/shard_map/while/body/eval_jaxpr/jit(_take)/select_n | solution.py:112
  202.6 9.0 %copy.96 = bf16[8,8,64,8,128]{4,2,1,3,0:T(8,128)(2,1)} copy(bf16[8,8,64,8,128]{4,3,2,1,0:T(8,128)(2,1)} %get-tuple-element.253) | data formatting | bytes 16777216 | tf_op jit(solution)/shard_map/while/body/eval_jaxpr/jit(_take)/select_n | solution.py:112
  211.7 9.6 %fusion.107 = f32[8,8,64,512]{3,2,1,0:T(8,128)} fusion(bf16[8,512,8,128]{3,1,2,0:T(8,128)(2,1)} %bitcast.133, bf16[1,8,64,8,128]{4,3,2,1,0:T(8,128)(2,1)S(1)} %constant_dynamic-slice_fusion.6), kind=kOutput, calls=%fused_computation.57.clone.1 | convolution fusion | flops 536870912 | bytes 17825792 | tf_op jit(solution)/shard_map/while/body/eval_jaxpr/pqhs,pkhs->phqk/dot_general | solution.py:118
  221.5 11.4 %fusion.108 = (f32[8,8,64]{2,1,0:T(8,128)S(1)}, f32[8,8,64,512]{3,2,1,0:T(8,128)}) fusion(f32[8,8,64,512]{3,2,1,0:T(8,128)} %fusion.107, pred[8,512]{1,0:T(8,128)(4,1)S(1)} %broadcast_in_dim.104), kind=kOutput, calls=%fused_computation.83.clone.1 | output fusion | flops 12583423 | bytes 16797696 | tf_op jit(solution)/shard_map/while/body/eval_jaxpr/sub | solution.py:26
  232.9 9.0 %copy.95 = bf16[8,8,64,8,128]{4,2,1,3,0:T(8,128)(2,1)} copy(bf16[8,8,64,8,128]{4,3,2,1,0:T(8,128)(2,1)} %get-tuple-element.252) | data formatting | bytes 16777216 | tf_op jit(solution)/shard_map/while/body/eval_jaxpr/jit(_take)/select_n | solution.py:115
  241.8 8.3 %fusion.109 = bf16[2,8,64,8,128]{4,2,3,1,0:T(8,128)(2,1)} fusion(bf16[2,8,64,8,128]{4,2,3,1,0:T(8,128)(2,1)} %get-tuple-element.265, s32[]{:T(128)} %get-tuple-element.264, bf16[8,512,8,128]{3,1,2,0:T(8,128)(2,1)} %bitcast.137, f32[8,8,64,512]{3,2,1,0:T(8,128)} %get-tuple-element.254, f32[8,8,64]{2,1,0:T(8,128)S(1)} %get-tuple-element.255), kind=kOutput, calls=%fused_computation.55.clone.1 | convolution fusion | flops 541589504 | bytes 17842688 | tf_op jit(solution)/shard_map/while/body/eval_jaxpr/phqk,pkhs->pqhs/dot_general | solution.py:124
  250.3 7.6 %gather_fusion = bf16[64,64,8,128]{3,2,1,0:T(8,128)(2,1)} fusion(bf16[32,64,8,128]{3,2,1,0:T(8,128)(2,1)} %get-tuple-element.278, s32[1024]{0:T(1024)S(1)} %pad_clamp_fusion.2), kind=kCustom, calls=%fused_computation.1.clone.clone.1 | custom fusion | bytes 16777472 | tf_op jit(solution)/shard_map/while/body/eval_jaxpr/jit(_take)/gather | solution.py:112
  258.0 7.6 %gather_fusion.1 = bf16[64,64,8,128]{3,2,1,0:T(8,128)(2,1)} fusion(bf16[32,64,8,128]{3,2,1,0:T(8,128)(2,1)} %get-tuple-element.275, s32[1024]{0:T(1024)S(1)} %pad_clamp_fusion.2), kind=kCustom, calls=%fused_computation.clone.clone.1 | custom fusion | bytes 16777472 | tf_op jit(solution)/shard_map/while/body/eval_jaxpr/jit(_take)/gather | solution.py:115
  265.6 11.6 %broadcast_select_fusion.3 = (bf16[8,8,64,8,128]{4,3,2,1,0:T(8,128)(2,1)}, bf16[8,8,64,8,128]{4,3,2,1,0:T(8,128)(2,1)}) fusion(bf16[8,8,64,8,128]{4,3,2,1,0:T(8,128)(2,1)} %bitcast.131, pred[8,8]{1,0:T(8,128)(4,1)S(1)} %compare_and_fusion.2, bf16[8,8,64,8,128]{4,3,2,1,0:T(8,128)(2,1)} %bitcast.132), kind=kLoop, calls=%fused_computation.46.clone.1 | loop fusion | flops 8388608 | bytes 33554496 | tf_op jit(solution)/shard_map/while/body/eval_jaxpr/jit(_take)/select_n | solution.py:112
  277.2 9.0 %copy.96 = bf16[8,8,64,8,128]{4,2,1,3,0:T(8,128)(2,1)} copy(bf16[8,8,64,8,128]{4,3,2,1,0:T(8,128)(2,1)} %get-tuple-element.253) | data formatting | bytes 16777216 | tf_op jit(solution)/shard_map/while/body/eval_jaxpr/jit(_take)/select_n | solution.py:112
  286.3 9.6 %fusion.107 = f32[8,8,64,512]{3,2,1,0:T(8,128)} fusion(bf16[8,512,8,128]{3,1,2,0:T(8,128)(2,1)} %bitcast.133, bf16[1,8,64,8,128]{4,3,2,1,0:T(8,128)(2,1)S(1)} %constant_dynamic-slice_fusion.6), kind=kOutput, calls=%fused_computation.57.clone.1 | convolution fusion | flops 536870912 | bytes 17825792 | tf_op jit(solution)/shard_map/while/body/eval_jaxpr/pqhs,pkhs->phqk/dot_general | solution.py:118
  296.1 11.4 %fusion.108 = (f32[8,8,64]{2,1,0:T(8,128)S(1)}, f32[8,8,64,512]{3,2,1,0:T(8,128)}) fusion(f32[8,8,64,512]{3,2,1,0:T(8,128)} %fusion.107, pred[8,512]{1,0:T(8,128)(4,1)S(1)} %broadcast_in_dim.104), kind=kOutput, calls=%fused_computation.83.clone.1 | output fusion | flops 12583423 | bytes 16797696 | tf_op jit(solution)/shard_map/while/body/eval_jaxpr/sub | solution.py:26
  307.5 9.0 %copy.95 = bf16[8,8,64,8,128]{4,2,1,3,0:T(8,128)(2,1)} copy(bf16[8,8,64,8,128]{4,3,2,1,0:T(8,128)(2,1)} %get-tuple-element.252) | data formatting | bytes 16777216 | tf_op jit(solution)/shard_map/while/body/eval_jaxpr/jit(_take)/select_n | solution.py:115
  316.4 8.3 %fusion.109 = bf16[2,8,64,8,128]{4,2,3,1,0:T(8,128)(2,1)} fusion(bf16[2,8,64,8,128]{4,2,3,1,0:T(8,128)(2,1)} %get-tuple-element.265, s32[]{:T(128)} %get-tuple-element.264, bf16[8,512,8,128]{3,1,2,0:T(8,128)(2,1)} %bitcast.137, f32[8,8,64,512]{3,2,1,0:T(8,128)} %get-tuple-element.254, f32[8,8,64]{2,1,0:T(8,128)S(1)} %get-tuple-element.255), kind=kOutput, calls=%fused_computation.55.clone.1 | convolution fusion | flops 541589504 | bytes 17842688 | tf_op jit(solution)/shard_map/while/body/eval_jaxpr/phqk,pkhs->pqhs/dot_general | solution.py:124
  324.7 17.7 %conditional.3 = (bf16[16,64,8,128]{3,1,2,0:T(8,128)(2,1)}) conditional(s32[]{:T(128)} %convert_element_type.33, bf16[16,64,8,128]{3,1,2,0:T(8,128)(2,1)} %get-tuple-element.280, (s32[]{:T(128)}, s32[]{:T(128)}, pred[]{:T(512)}, s32[]{:T(128)}, bf16[16,64,8,128]{3,2,1,0:T(8,128)(2,1)S(1)}, /*index=5*/bf16[2048,8,128]{2,1,0:T(8,128)(2,1)}, ...), branch_computations={%region_8.10_spmd, %region_9.13_spmd} | conditional | flops 812716544 | bytes 50729176 | solution.py:151
  344.4 76.1 %all_to_all.44 = bf16[16,64,1024]{2,1,0:T(8,128)(2,1)S(1)} all-to-all(bf16[16,64,1024]{2,1,0:T(8,128)(2,1)S(1)} %copy_bitcast_fusion.2), channel_id=1, replica_groups=mesh['groups'=2,'seq'=16] {'seq'}, dimensions={0} | all-to-all | bytes 4194304 | tf_op jit(solution)/shard_map/all_to_all | solution.py:152
  (76 shorter events, 66.3 us)
Async XLA Ops:
  0.0 122.1 %copy-start = (s32[2,32,3]{1,0,2:T(2,128)S(1)}, s32[2,32,3]{1,0,2:T(2,128)}, u32[]{:S(2)}) copy-start(s32[2,32,3]{1,0,2:T(2,128)} %param.16) | copy-start | bytes 2308
  5.3 49.0 %all-to-all-start = ((bf16[16,64,1024]{2,1,0:T(8,128)(2,1)}), bf16[16,64,1024]{2,1,0:T(8,128)(2,1)}, u32[]{:S(2)}, u32[]{:S(2)}) async-start(bf16[16,64,1024]{2,1,0:T(8,128)(2,1)} %bitcast.19), calls=%async_computation | async-start | bytes 4194304 | tf_op jit(solution)/shard_map/all_to_all | solution.py:59
  54.3 52.3 %all-to-all-start.2 = ((bf16[16,64,1024]{2,1,0:T(8,128)(2,1)}), bf16[16,64,1024]{2,1,0:T(8,128)(2,1)}, u32[]{:S(2)}, u32[]{:S(2)}) async-start(bf16[16,64,1024]{2,1,0:T(8,128)(2,1)} %bitcast.26), calls=%async_computation.2 | async-start | bytes 4194304 | tf_op jit(solution)/shard_map/all_to_all | solution.py:58
  68.3 49.5 %copy-start.7 = (s32[2,2]{1,0:T(2,128)S(1)}, s32[2,2]{1,0:T(2,128)}, u32[]{:S(2)}) copy-start(s32[2,2]{1,0:T(2,128)} %param.17) | copy-start | bytes 52
  106.6 52.2 %all-to-all-start.1 = ((bf16[16,64,1024]{2,1,0:T(8,128)(2,1)}), bf16[16,64,1024]{2,1,0:T(8,128)(2,1)S(1)}, u32[]{:S(2)}, u32[]{:S(2)}) async-start(bf16[16,64,1024]{2,1,0:T(8,128)(2,1)} %bitcast.24), calls=%async_computation.1 | async-start | bytes 4194304 | tf_op jit(solution)/shard_map/all_to_all | solution.py:57
  117.2 45.1 %collective-permute-start = (bf16[1,1024,1024]{2,1,0:T(8,128)(2,1)}, bf16[1,1024,1024]{2,1,0:T(8,128)(2,1)}, u32[]{:S(2)}, u32[]{:S(2)}) collective-permute-start(bf16[1,1024,1024]{2,1,0:T(8,128)(2,1)} %bitcast.21), channel_id=1, source_target_pairs={{0,1},{1,0},{2,3},{3,2},{4,5},{5,4},{6,7},{7,6},{8,9},{9,8},{10,11... | collective-permute-start | bytes 6291464 | tf_op jit(solution)/shard_map/ppermute | solution.py:21
  117.4 45.0 %collective-permute-start.1 = (bf16[1,1024,1024]{2,1,0:T(8,128)(2,1)}, bf16[1,1024,1024]{2,1,0:T(8,128)(2,1)}, u32[]{:S(2)}, u32[]{:S(2)}) collective-permute-start(bf16[1,1024,1024]{2,1,0:T(8,128)(2,1)} %bitcast.28), channel_id=1, source_target_pairs={{0,1},{1,0},{2,3},{3,2},{4,5},{5,4},{6,7},{7,6},{8,9},{9,8},{10,11... | collective-permute-start | bytes 6291464 | tf_op jit(solution)/shard_map/ppermute | solution.py:21
  158.8 1.4 copy-start.4
  325.3 2.9 copy-start.3
  325.9 1.3 copy-start.6
  420.5 4.4 %copy-start.1 = (s32[2,32,3]{1,0,2:T(2,128)S(1)}, s32[2,32,3]{1,0,2:T(2,128)}, u32[]{:S(2)}) copy-start(s32[2,32,3]{1,0,2:T(2,128)} %param.16) | copy-start | bytes 2308
where the time goes:
time: 426 us; the launch traced here: 425 us
  waiting for transfers between devices  108 us (25%)
  local copies, waits for them, and re-layouts  104 us (24%)
  blocking collectives  76.1 us (18%)
  other arithmetic  53.2 us (12%)
  matrix products  50.1 us (12%)
  starting transfers between devices  29.2 us (7%)
    all_to_all x1, blocking collectives, per_device(): lax.all_to_all(attended.reshape(devices, block_len, group_width), 'seq',...  76.1 us
    all_to_all x1, waiting for transfers between devices, per_device(): lax.all_to_all(by_parity(value_states), 'seq', split_axis=0, concat_axis=...  36.3 us
    all_to_all x1, waiting for transfers between devices, per_device(): lax.all_to_all(by_parity(key_states), 'seq', split_axis=0, concat_axis=1,...  36.3 us
    all_to_all x1, waiting for transfers between devices, per_device(): lax.all_to_all(by_parity(queries), 'seq', split_axis=0, concat_axis=1, ti...  35.8 us
    select_n x2, other arithmetic, local_group(): jnp.take(key_blocks, listed_group, axis=0)  23.2 us
    sub x2, other arithmetic, soft_weights(): exponent = jnp.exp(scores - row_max)  22.8 us
    dot_general x2, matrix products, local_group(): jnp.einsum('pqhs,pkhs->phqk', query_group, gathered_keys, preferred_eleme...  19.2 us
    select_n x2, local copies, waits for them, and re-layouts, local_group(): jnp.take(key_blocks, listed_group, axis=0)  17.9 us
  transfers between devices with their start and end apart: 5, of which 3 were waited for; matrix products, arithmetic and copies ran while one was open for 3% of the time, Pallas kernels for 0%

commit v1 on v0

--- a/solution.py
+++ b/solution.py
@@ -1,8 +1,11 @@
+import functools
 import math
 
 import jax
 import jax.numpy as jnp
 from jax import lax
+from jax.experimental import pallas as pl
+from jax.experimental.pallas import tpu as pltpu
 from jax.sharding import PartitionSpec as P
 
 HEAD_DIM = 128
@@ -162,6 +165,214 @@
     return returned.reshape(documents, 2 * block_len, head_groups * group_width)
 
 
+SCALE = HEAD_DIM ** (-0.5)
+MESH = pl.DeviceIdType.MESH
+
+
+def fused_kernel(
+    devices, heads_here, random_ref, global_ref, q_in, k_in, v_in, out_ref,
+    q_buf, k_buf, v_buf, o_buf, wide_rows, in_send, in_recv, out_send, out_recv, own_sem,
+):
+    documents, blocks_here, _, width = q_in.shape
+    chunks = documents * heads_here
+    total_blocks = devices * blocks_here
+    half = devices // 2
+    me = lax.axis_index("seq")
+    side = me // half
+
+    def partner(step):
+        return (side + 1 + step // half) % 2 * half + (me + step) % half
+
+    barrier = pltpu.get_barrier_semaphore()
+
+    def greet(step, carry):
+        @pl.when(step != half)
+        def _():
+            pl.semaphore_signal(barrier, inc=1, device_id={"seq": partner(step)}, device_id_type=MESH)
+
+        return carry
+
+    arrays = ((q_in, q_buf), (k_in, k_buf), (v_in, v_buf))
+
+    def own_in(chunk, index):
+        source, target = arrays[index]
+        column = pl.multiple_of((me * heads_here + chunk % heads_here) * HEAD_DIM, HEAD_DIM)
+        return pltpu.make_async_copy(
+            source.at[chunk // heads_here, :, :, pl.ds(column, HEAD_DIM)],
+            target.at[chunk, pl.ds(me * blocks_here, blocks_here)],
+            own_sem.at[index, chunk],
+        )
+
+    def own_out(chunk):
+        column = pl.multiple_of((me * heads_here + chunk % heads_here) * HEAD_DIM, HEAD_DIM)
+        return pltpu.make_async_copy(
+            o_buf.at[chunk, pl.ds(me * blocks_here, blocks_here)],
+            out_ref.at[chunk // heads_here, :, :, pl.ds(column, HEAD_DIM)],
+            own_sem.at[3, chunk],
+        )
+
+    def send_in(place, carry):
+        chunk, step = place // devices, place % devices
+
+        @pl.when(step != half)
+        def _():
+            target_device = partner(step)
+            column = pl.multiple_of(
+                (target_device * heads_here + chunk % heads_here) * HEAD_DIM, HEAD_DIM
+            )
+            for index, (source, target) in enumerate(arrays):
+                pltpu.make_async_remote_copy(
+                    src_ref=source.at[chunk // heads_here, :, :, pl.ds(column, HEAD_DIM)],
+                    dst_ref=target.at[chunk, pl.ds(me * blocks_here, blocks_here)],
+                    send_sem=in_send.at[index],
+                    recv_sem=in_recv.at[index, chunk],
+                    device_id={"seq": target_device},
+                    device_id_type=MESH,
+                ).start()
+
+        return carry
+
+    for chunk in range(chunks):
+        for index in range(3):
+            own_in(chunk, index).start()
+    lax.fori_loop(0, devices, greet, 0)
+    pl.semaphore_wait(barrier, devices - 1)
+    lax.fori_loop(0, chunks * devices, send_in, 0)
+
+    other_blocks = (devices - 1) * blocks_here
+    lanes = lax.broadcasted_iota(jnp.int32, (1, (NGLOB + 3 + NRAND) * BLOCK), 1) // BLOCK
+
+    def arrived(ref, send_sem, recv_sem):
+        return pltpu.make_async_remote_copy(
+            src_ref=ref, dst_ref=ref, send_sem=send_sem, recv_sem=recv_sem,
+            device_id={"seq": partner(0)}, device_id_type=MESH,
+        )
+
+    def softmax_values(scores, values):
+        row_max = jnp.max(scores, axis=-1, keepdims=True)
+        exponent = jnp.exp((scores - row_max) * SCALE)
+        total = jnp.sum(exponent, axis=-1, keepdims=True)
+        mixed = jnp.dot(exponent.astype(jnp.bfloat16), values, preferred_element_type=jnp.float32)
+        return (mixed / total).astype(jnp.bfloat16)
+
+    def products(left, right):
+        return lax.dot_general(
+            left, right, (((1,), (1,)), ((), ())), preferred_element_type=jnp.float32
+        )
+
+    def block_at(ref, chunk, block):
+        return ref[chunk, block]
+
+    def attend(chunk, carry):
+        document = chunk // heads_here
+        globals_here = [global_ref[document, slot] for slot in range(NGLOB)]
+        for slot in range(NGLOB):
+            wide_rows[slot] = softmax_values(
+                products(block_at(q_buf, chunk, globals_here[slot]), k_buf[chunk].reshape(-1, HEAD_DIM)),
+                v_buf[chunk].reshape(-1, HEAD_DIM),
+            )
+
+        def owner(step, inner):
+            target_device = partner(step)
+            for offset in range(blocks_here):
+                block = target_device * blocks_here + offset
+                listed = globals_here + [
+                    jnp.maximum(block - 1, 0), block, jnp.minimum(block + 1, total_blocks - 1)
+                ] + [
+                    random_ref[document, block * NRAND + pick] for pick in range(NRAND)
+                ]
+                keys = jnp.concatenate([block_at(k_buf, chunk, item) for item in listed], axis=0)
+                values = jnp.concatenate([block_at(v_buf, chunk, item) for item in listed], axis=0)
+                scores = products(block_at(q_buf, chunk, block), keys)
+                dead = ((lanes == NGLOB) & (block == 0)) | (
+                    (lanes == NGLOB + 2) & (block == total_blocks - 1)
+                )
+                mixed = softmax_values(jnp.where(dead, -1e30, scores), values)
+                for slot in range(NGLOB):
+                    mixed = jnp.where(
+                        jnp.full(mixed.shape, globals_here[slot]) == block, wide_rows[slot], mixed
+                    )
+                o_buf[chunk, block] = mixed
+
+            @pl.when(step != half)
+            def _():
+                column = pl.multiple_of(
+                    (me * heads_here + chunk % heads_here) * HEAD_DIM, HEAD_DIM
+                )
+                pltpu.make_async_remote_copy(
+                    src_ref=o_buf.at[chunk, pl.ds(target_device * blocks_here, blocks_here)],
+                    dst_ref=out_ref.at[document, :, :, pl.ds(column, HEAD_DIM)],
+                    send_sem=out_send,
+                    recv_sem=out_recv,
+                    device_id={"seq": target_device},
+                    device_id_type=MESH,
+                ).start()
+
+            @pl.when(step == half)
+            def _():
+                own_out(chunk).start()
+
+            return inner
+
+        lax.fori_loop(0, devices, owner, 0)
+        return carry
+
+    for chunk in range(chunks):
+        for index, (source, target) in enumerate(arrays):
+            own_in(chunk, index).wait()
+            arrived(
+                target.at[chunk, pl.ds(0, other_blocks)], in_send.at[index], in_recv.at[index, chunk]
+            ).wait_recv()
+    lax.fori_loop(0, chunks, attend, 0)
+    other_width = (devices - 1) * (width // devices)
+    for chunk in range(chunks):
+        own_out(chunk).wait()
+    for index, (source, target) in enumerate(arrays):
+        arrived(
+            source.at[:, :, :, pl.ds(0, other_width)], in_send.at[index], in_recv.at[index, 0]
+        ).wait_send()
+    arrived(o_buf.at[:, pl.ds(0, other_blocks)], out_send, out_recv).wait_send()
+    arrived(out_ref.at[:, :, :, pl.ds(0, other_width)], out_send, out_recv).wait_recv()
+
+
+def fused(queries, key_states, value_states, random_blocks, global_blocks):
+    devices = lax.axis_size("seq")
+    documents, rows, width = queries.shape
+    heads_here = width // HEAD_DIM // devices
+    chunks = documents * heads_here
+    blocked = (documents, rows // BLOCK, BLOCK, width)
+    gathered = pltpu.VMEM((chunks, devices * rows // BLOCK, BLOCK, HEAD_DIM), jnp.bfloat16)
+    anywhere = pl.BlockSpec(memory_space=pl.ANY)
+    scalars = pl.BlockSpec(memory_space=pltpu.SMEM)
+    return pl.pallas_call(
+        functools.partial(fused_kernel, devices, heads_here),
+        out_shape=jax.ShapeDtypeStruct(blocked, queries.dtype),
+        in_specs=[scalars, scalars, anywhere, anywhere, anywhere],
+        out_specs=anywhere,
+        scratch_shapes=[
+            gathered, gathered, gathered, gathered,
+            pltpu.VMEM((NGLOB, BLOCK, HEAD_DIM), jnp.bfloat16),
+            pltpu.SemaphoreType.DMA((3,)),
+            pltpu.SemaphoreType.DMA((3, chunks)),
+            pltpu.SemaphoreType.DMA,
+            pltpu.SemaphoreType.DMA,
+            pltpu.SemaphoreType.DMA((4, chunks)),
+        ],
+        compiler_params=pltpu.CompilerParams(collective_id=0, has_side_effects=True),
+    )(
+        random_blocks.reshape(documents, -1), global_blocks,
+        queries.reshape(blocked), key_states.reshape(blocked), value_states.reshape(blocked),
+    ).reshape(queries.shape)
+
+
+def per_device_any(queries, key_states, value_states, random_blocks, global_blocks):
+    devices = lax.axis_size("seq")
+    heads = queries.shape[2] // HEAD_DIM
+    if devices % 2 == 0 and heads % devices == 0 and queries.shape[1] % BLOCK == 0:
+        return fused(queries, key_states, value_states, random_blocks, global_blocks)
+    return per_device(queries, key_states, value_states, random_blocks, global_blocks)
+
+
 def solution(mesh):
     placed = (
         P("groups", "seq", None),
@@ -171,5 +382,5 @@
         P("groups", None),
     )
     return jax.shard_map(
-        per_device, mesh=mesh, in_specs=placed, out_specs=P("groups", "seq", None), check_vma=False
-    )
+        per_device_any, mesh=mesh, in_specs=placed, out_specs=P("groups", "seq", None), check_vma=False
+    )

time: 426 us -> 204 us (0.48)
  Pallas kernels: 0 us -> 199 us
  waiting for transfers between devices: 108 us -> 0 us
  local copies, waits for them, and re-layouts: 104 us -> 4.57 us
  blocking collectives: 76.1 us -> 0 us
  other arithmetic: 53.2 us -> 0 us
  matrix products: 50.1 us -> 0 us
  starting transfers between devices: 29.2 us -> 0 us
    pallas_call x0 -> x1, Pallas kernels: none -> 199 us  [fused(): pl.pallas_call(functools.partial(fused_kernel, devices, heads_here), out_...]
    all_to_all x3 -> x0, waiting for transfers between devices: 108 us -> none  [the longest x1 36.3 us: per_device(): lax.all_to_all(by_parity(value_states), 'seq', split_axis=0, concat_axis=...]
    all_to_all x1 -> x0, blocking collectives: 76.1 us -> none  [per_device(): lax.all_to_all(attended.reshape(devices, block_len, group_width), 'seq',...]
    dot_general x6 -> x0, matrix products: 45.5 us -> none  [the longest x2 19.2 us: local_group(): jnp.einsum('pqhs,pkhs->phqk', query_group, gathered_keys, preferred_eleme...]
    select_n x4 -> x0, local copies, waits for them, and re-layouts: 35.9 us -> none  [the longest x2 17.9 us: local_group(): jnp.take(key_blocks, listed_group, axis=0)]
    gather x4 -> x0, local copies, waits for them, and re-layouts: 30.5 us -> none  [the longest x2 15.3 us: local_group(): jnp.take(key_blocks, listed_group, axis=0)]
    select_n x5 -> x0, other arithmetic: 30.3 us -> none  [the longest x2 23.2 us: local_group(): jnp.take(key_blocks, listed_group, axis=0)]
    all_to_all x3 -> x0, starting transfers between devices: 28.7 us -> none  [the longest x1 10.7 us: per_device(): lax.all_to_all(by_parity(key_states), 'seq', split_axis=0, concat_axis=1,...]
  transfers between devices with their start and end apart: 5 -> 0, of which waited for: 3 -> 0; matrix products, arithmetic and copies ran while one was open for 3% -> 0% of each run, Pallas kernels for 0% -> 0%
where the time goes in v1:
time: 204 us
  Pallas kernels  199 us (98%)
  local copies, waits for them, and re-layouts  4.57 us (2%)
    pallas_call x1, Pallas kernels, fused(): pl.pallas_call(functools.partial(fused_kernel, devices, heads_here), out_...  199 us

profile of v1, /device:TPU:1, one launch (start us, length us, event | category | flops | bytes accessed | tf_op | source)
XLA Modules:
  0.0 203.9 jit_solution(2306421662667736174)
XLA Ops:
  0.0 0.8 copy.7
  0.8 0.7 reshape.15.random_ref
  1.4 199.3 %shard_map.55 = bf16[2,2,64,4096]{3,2,1,0:T(8,128)(2,1)} custom-call(s32[2,96]{1,0:T(2,128)} %reshape.15.random_ref, s32[2,2]{1,0:T(2,128)} %global_ref.1, bf16[2,2,64,4096]{3,2,1,0:T(8,128)(2,1)} %bitcast.5, bf16[2,2,64,4096]{3,2,1,0:T(8,128)(2,1)} %bitcast.6, bf16[2,2,64,4096]{3,2,1,0:T(8,128)(2,1)} %bitcast.7), custom_call_target="tpu_custom_call" | custom-call | tf_op jit(solution)/shard_map/pallas_call | solution.py:347
  200.8 3.1 %copy.9 = bf16[2,128,4096]{2,1,0:T(8,128)(2,1)} copy(bf16[2,128,4096]{2,1,0:T(8,128)(2,1)} %bitcast.4) | data formatting | bytes 4194304
